TPU v7x, 32 devices: a whole 2x2x4 slice. The times are simulated.
32 devices in a mesh: gx: 8 (over z, y), gy: 4 (over x, core).
Axes of the slice: x: 2, y: 2, z: 4, core: 2. Of those that a mesh axis runs over, the one named last changes fastest.
Arguments:
- positions: float32 [3, 131072], P(None, ('gx', 'gy')), may hold values from 0 to 128, as said below
- mass: float32 [131072], P(('gx', 'gy')), may hold values from 0.5 to 2
- smoothing: float32 [131072], P(('gx', 'gy')), may hold values from 1.5 to 3
- energy: float32 [131072], P(('gx', 'gy')), may hold values from 0.5 to 4
- destination: int32 [131072, 1], P(('gx', 'gy')), may hold values from 0 to 31, as said below
- pairs: int32 [2, 27648], P(None, ('gx', 'gy')), may hold values from 0 to 63, as said below
- pair_count: int32 [32], P(('gx', 'gy')), may hold values from 432 to 864, as said below
Outputs:
- density: float32 [131072], P(('gx', 'gy'))
- accel: float32 [3, 131072], P(None, ('gx', 'gy'))
Inputs may be any that keep to these rules, and one draw needn't show every extreme that they name: `destination`: the 4096 particles of every domain name each domain exactly 128 times. `positions`: each particle lies in the box of its new domain (i, j): first coordinate in [16 i, 16 (i + 1)], second in [16 j, 16 (j + 1)], third in [0, 16]. `pairs`: row 0 holds target tiles below 32, row 1 source tiles below 32 + 4 * 8 (tiles from 32 on are ghost tiles); domain d's list is columns d * 864 to (d + 1) * 864 - 1, and slots from pair_count[d] on are unused. `pair_count`: some domain uses all 864 slots.
All inputs are finite; a program needn't handle non-finite values.
Results may differ from a plain program's by a relative error of at most 0.0005.
Values sent between devices are 32-bit elements; how exact they have to be, the bound alone decides.
A program may use at most 64 MiB of HBM per device.

v0:
```python
import functools
import math

import jax
import jax.numpy as jnp
from jax import lax
from jax.experimental import pallas as pl
from jax.experimental.pallas import tpu as pltpu
from jax.sharding import PartitionSpec as P

GT = 8
LANES = 128
FEATS = 32
TINY = 1e-12

KERNEL_NORM = 21.0 / (2.0 * math.pi)
GAMMA_LESS = 2.0 / 3.0


def extended(block, sides, width):
    for axis, dim in sides:
        count = lax.axis_size(axis)
        forward = [(i, i + 1) for i in range(count - 1)]
        backward = [(target, source) for source, target in forward]
        low = lax.ppermute(
            lax.slice_in_dim(block, block.shape[dim] - width, None, axis=dim), axis, forward
        )
        high = lax.ppermute(lax.slice_in_dim(block, 0, width, axis=dim), axis, backward)
        block = jnp.concatenate([low, block, high], axis=dim)
    return block


def neighbour_rows(ghosts):
    return jnp.concatenate(
        [ghosts[..., 0, 1, :], ghosts[..., 2, 1, :], ghosts[..., 1, 0, :], ghosts[..., 1, 2, :]],
        axis=-1,
    )


def three(x):
    one = x.astype(jnp.bfloat16).astype(jnp.float32)
    rest = x - one
    two = rest.astype(jnp.bfloat16).astype(jnp.float32)
    return one, two, (rest - two).astype(jnp.bfloat16).astype(jnp.float32)


def source_terms(x):
    one, two, low = three(x)
    return [one, two, one, two, low, one]


def target_terms(x):
    one, two, low = three(x)
    return [one, one, two, two, one, low]


def put_rows(stage, rows, width, tiles):
    for k, row in enumerate(rows):
        stage[pl.ds(k, tiles, stride=width), :] = row


def plan_kernel(count_ref, pairs_ref, sizes_ref, own_ref, ghost_ref, times_ref, own_tiles, tiles):
    step = 16

    def clear(block, carry):
        for u in range(step):
            times_ref[block * step + u] = 0
        return carry

    lax.fori_loop(0, times_ref.shape[0] // step, clear, 0)

    count = count_ref[0]
    spare = own_tiles * tiles
    last = pairs_ref.shape[1] - 1
    ahead = 8

    def add(block, carry):
        own, ghost = carry
        picked = []
        for u in range(ahead):
            k = block * ahead + u
            live = k < count
            at = jnp.minimum(k, last)
            source = jnp.where(live, pairs_ref[1, at], 0)
            key = jnp.where(live, pairs_ref[0, at] * tiles + source, spare)
            near = (source < own_tiles).astype(jnp.int32)
            alive = live.astype(jnp.int32)
            picked.append((key, near * alive, (1 - near) * alive))
        for key, near, beyond in picked:
            seen = times_ref[key]
            times_ref[key] = seen + 1
            own_ref[own] = key
            ghost_ref[ghost] = key
            fresh = (seen == 0).astype(jnp.int32)
            own = own + fresh * near
            ghost = ghost + fresh * beyond
        return own, ghost

    own, ghost = lax.fori_loop(0, (count + ahead - 1) // ahead, add, (0, 0))
    sizes_ref[0] = own
    sizes_ref[1] = ghost


def one_hot_rows(dest):
    rows = lax.broadcasted_iota(jnp.int32, (LANES, LANES), 0)
    wide = jnp.broadcast_to(dest, (LANES, LANES))
    return jnp.where(wide == rows, 1.0, 0.0).astype(jnp.bfloat16)


def by_last(a, b):
    return lax.dot_general(a, b, (((1,), (1,)), ((), ())), preferred_element_type=jnp.float32)


def sweep(list_ref, size, times_ref, tiles, dump, unroll, body):
    last = list_ref.shape[0] - 1

    def advance(block, carry):
        for u in range(unroll):
            k = block * unroll + u
            live = k < size
            key = jnp.where(live, list_ref[jnp.minimum(k, last)], 0)
            target = key // tiles
            source = key - target * tiles
            weight = times_ref[key].astype(jnp.float32)
            body(target, source, jnp.where(live, target, dump), weight)
        return carry

    lax.fori_loop(0, (size + unroll - 1) // unroll, advance, 0)


def keep_rows(stage, near, tiles):
    group = 4

    def keep(block, carry):
        for u in range(group):
            t = block * group + u
            near[t] = stage[pl.ds(t * FEATS, FEATS), :].astype(jnp.bfloat16)
        return carry

    lax.fori_loop(0, tiles // group, keep, 0)


def target_rows(coords, scale, stage, near, tiles):
    norm = sum(c * c for c in coords)
    zero = jnp.zeros_like(norm)
    rows = []
    for c in coords:
        rows += target_terms(-2.0 * c * scale)
    rows += target_terms(scale)
    rows += list(three(norm * scale))
    rows += [zero] * (FEATS - len(rows))
    put_rows(stage, rows, FEATS, tiles)
    keep_rows(stage, near, tiles)


def spread_column(far, first, last, wide):
    row = lax.broadcasted_iota(jnp.int32, (FEATS, LANES), 0)
    pick = jnp.where((row >= first) & (row < last), 1.0, 0.0).astype(jnp.bfloat16)
    group = 4

    def one(block, carry):
        for u in range(group):
            t = block * group + u
            wide[t] = jnp.dot(far[t], pick, preferred_element_type=jnp.float32)
        return carry

    lax.fori_loop(0, wide.shape[0] // group, one, 0)


def density_kernel(sizes_ref, own_ref, ghost_ref, times_ref, pool_ref,
                   dens_ref, press_ref, far, packed_ref, dest_ref, more_ref,
                   stage, near, mass_b, totals):
    own_tiles = dens_ref.shape[0]
    tiles = pool_ref.shape[1]
    ghosts = tiles - own_tiles
    own, out_of_reach = [], 0.0
    ghost = []
    reach = jnp.max(pool_ref[4]) + 0.01
    for k in range(3):
        x = pool_ref[k, :own_tiles]
        low, high = jnp.min(x), jnp.max(x)
        centre = 0.5 * (low + high)
        far_x = pool_ref[k, own_tiles:]
        gap = jnp.maximum(jnp.maximum(low - far_x, far_x - high), 0.0)
        out_of_reach = out_of_reach + gap * gap
        own.append(x - centre)
        ghost.append(far_x - centre)
    ghost_mass = pool_ref[3, own_tiles:]
    active = (out_of_reach < reach * reach) & (ghost_mass != 0.0)
    upto = lax.broadcasted_iota(jnp.int32, (LANES, LANES), 0) <= lax.broadcasted_iota(
        jnp.int32, (LANES, LANES), 1)
    upto = jnp.where(upto, 1.0, 0.0).astype(jnp.bfloat16)
    flags = jnp.where(active, 1.0, 0.0).astype(jnp.bfloat16)
    rank = jnp.dot(flags, upto, preferred_element_type=jnp.float32)
    dest = jnp.where(active, rank - 1.0, -1.0).astype(jnp.int32)
    dest_ref[...] = dest
    most = jnp.max(rank)
    more = (most > LANES // 2 + 0.5).astype(jnp.int32)
    more_ref[0] = more
    split = [three(x) for x in ghost + [ghost_mass, pool_ref[4, own_tiles:]]]
    zero = jnp.zeros_like(ghost_mass)
    rows = []
    for term in range(3):
        rows += [s[term] for s in split] + [zero] * 3
    put_rows(stage, rows + [zero] * 8, FEATS, ghosts)

    def squeeze(block, carry):
        for u in range(4):
            g = block * 4 + u
            part = stage[pl.ds(g * FEATS, FEATS), :].astype(jnp.bfloat16)
            moved = by_last(part, one_hot_rows(dest_ref[pl.ds(g, 1), :]))
            totals[g] = moved[:8] + moved[8:16] + moved[16:24]
        return carry

    lax.fori_loop(0, ghosts // 4, squeeze, 0)
    fields = []
    for k, x in enumerate(own + [pool_ref[3, :own_tiles], pool_ref[4, :own_tiles]]):
        packed_ref[k, :own_tiles] = x
        packed_ref[k, own_tiles:] = totals[:ghosts, k, :]
        fields.append(packed_ref[k])
    norm = sum(c * c for c in fields[:3])
    ones = jnp.ones_like(norm)
    rows = []
    for c in fields[:3] + [norm]:
        rows += source_terms(c)
    rows += [ones, ones, ones] + list(three(0.5 * fields[4])) + list(three(fields[3])[:2])
    put_rows(stage, rows, FEATS, tiles)

    def turn(g, carry):
        for v in range(2):
            at = g * 2 + v
            cols = jnp.transpose(stage[pl.ds(at * LANES, LANES), :]).astype(jnp.bfloat16)
            for u in range(LANES // FEATS):
                far[at * (LANES // FEATS) + u] = cols[:, u * FEATS:(u + 1) * FEATS]
        return carry

    lax.fori_loop(0, tiles * FEATS // LANES // 2, turn, 0)
    radius = fields[4][:own_tiles]
    target_rows(own, 1.0 / (radius * radius), stage, near, own_tiles)
    spread_column(far, 30, 32, mass_b)
    totals[...] = jnp.zeros_like(totals)

    def add(first, height):
        def body(target, source, place, weight):
            sq = jnp.dot(far[source, first:first + height], near[target],
                         preferred_element_type=jnp.float32)
            sq = jnp.maximum(sq, TINY)
            ratio = sq * lax.rsqrt(sq)
            falloff = jnp.maximum(1.0 - ratio, 0.0)
            falloff = falloff * falloff
            term = falloff * falloff * ((ratio + 0.25) * mass_b[source, first:first + height])
            totals[place] += weight * jnp.sum(term.reshape(height // 8, 8, LANES), axis=0)
        return body

    half = LANES // 2
    sweep(own_ref, sizes_ref[0], times_ref, tiles, own_tiles, 4, add(0, LANES))
    sweep(ghost_ref, sizes_ref[1], times_ref, tiles, own_tiles, 8, add(0, half))

    @pl.when(more > 0)
    def _():
        sweep(ghost_ref, sizes_ref[1], times_ref, tiles, own_tiles, 4, add(half, half))

    summed = jnp.sum(totals[:own_tiles], axis=1)
    norm = KERNEL_NORM / (radius * radius * radius)
    density = norm * (4.0 * summed + pool_ref[3, :own_tiles])
    dens_ref[...] = density
    press_ref[...] = GAMMA_LESS * pool_ref[5, :own_tiles] / density


def accel_kernel(sizes_ref, own_ref, ghost_ref, times_ref, more_ref, far, packed_ref, dest_ref,
                 press_ref, press_far_ref, out_ref, stage, near, half_a, half_b, press_all, left, left_half,
                 totals):
    own_tiles = out_ref.shape[1]
    tiles = packed_ref.shape[1]
    ghosts = tiles - own_tiles
    half = LANES // 2
    zero = jnp.zeros((ghosts, LANES), jnp.float32)
    put_rows(stage, list(three(press_far_ref[...])) + [zero] * 13, 16, ghosts)

    def squeeze(block, carry):
        for u in range(4):
            g = block * 4 + u
            part = stage[pl.ds(g * 16, 16), :].astype(jnp.bfloat16)
            moved = by_last(part, one_hot_rows(dest_ref[pl.ds(g, 1), :]))
            press_all[pl.ds(own_tiles + g, 1), :] = moved[0:1] + moved[1:2] + moved[2:3]
        return carry

    lax.fori_loop(0, ghosts // 4, squeeze, 0)
    press_all[:own_tiles] = press_ref[...]
    own = [packed_ref[k, :own_tiles] for k in range(3)]
    target_rows(own, jnp.ones_like(own[0]), stage, near, own_tiles)
    spread_column(far, 27, 30, half_b)
    half_a[...] = 0.5 * packed_ref[4, :own_tiles]
    mass = packed_ref[3]
    load = mass * press_all[...]
    coords = [packed_ref[k] for k in range(3)]
    rows = [mass] + [mass * c for c in coords] + [load] + [load * c for c in coords]
    split = [three(row) for row in rows]
    put_rows(stage, [s[0] for s in split] + [s[1] for s in split], 16, tiles)

    def pack(block, carry):
        for u in range(4):
            t = block * 4 + u
            part = stage[pl.ds(t * 16, 16), :].astype(jnp.bfloat16)
            left[t] = jnp.concatenate([part, part], axis=1)
        return carry

    def pack_half(block, carry):
        for u in range(4):
            t = block * 4 + u
            part = stage[pl.ds((t + own_tiles) * 16, 16), :].astype(jnp.bfloat16)
            for v in range(2):
                piece = part[:, v * half:(v + 1) * half]
                left_half[v, t] = jnp.concatenate([piece, piece], axis=1)
        return carry

    lax.fori_loop(0, own_tiles // 4, pack, 0)
    lax.fori_loop(0, ghosts // 4, pack_half, 0)
    totals[...] = jnp.zeros_like(totals)

    def add(first, height, lhs):
        def body(target, source, place, weight):
            sq = jnp.dot(far[source, first:first + height], near[target],
                         preferred_element_type=jnp.float32)
            sq = jnp.maximum(sq, TINY)
            radius = half_b[source, first:first + height] + half_a[pl.ds(target, 1), :]
            dist = sq * lax.rsqrt(sq)
            guess = pl.reciprocal(radius, approx=True)
            inv = guess * (2.0 - radius * guess)
            fall = inv * jnp.maximum(1.0 - dist * inv, 0.0)
            wide = fall * inv
            slope = wide * wide * fall
            high = slope.astype(jnp.bfloat16)
            low = (slope - high.astype(jnp.float32)).astype(jnp.bfloat16)
            terms = jnp.concatenate([high, low], axis=0)
            totals[place] += weight * jnp.dot(lhs(source), terms, preferred_element_type=jnp.float32)
        return body

    sweep(own_ref, sizes_ref[0], times_ref, tiles, own_tiles, 4, add(0, LANES, lambda s: left[s]))
    sweep(ghost_ref, sizes_ref[1], times_ref, tiles, own_tiles, 8,
          add(0, half, lambda s: left_half[0, jnp.maximum(s - own_tiles, 0)]))

    @pl.when(more_ref[0] > 0)
    def _():
        sweep(ghost_ref, sizes_ref[1], times_ref, tiles, own_tiles, 4,
              add(half, half, lambda s: left_half[1, jnp.maximum(s - own_tiles, 0)]))

    folded = totals[:own_tiles, :8] + totals[:own_tiles, 8:]
    mixed = [press_ref[...] * folded[:, k] + folded[:, k + 4] for k in range(4)]
    for k in range(3):
        out_ref[k] = 20.0 * KERNEL_NORM * (own[k] * mixed[0] - mixed[k + 1])


SMEM = pl.BlockSpec(memory_space=pltpu.SMEM)
VMEM = pl.BlockSpec(memory_space=pltpu.VMEM)


def plan_call(count, pairs, own_tiles, tiles):
    slots = pairs.shape[1]
    shapes = [(2,), (slots + 1,), (slots + 1,), (own_tiles * tiles + LANES,)]
    return pl.pallas_call(
        functools.partial(plan_kernel, own_tiles=own_tiles, tiles=tiles),
        out_shape=[jax.ShapeDtypeStruct(shape, jnp.int32) for shape in shapes],
        in_specs=[SMEM, SMEM],
        out_specs=[SMEM] * 4,
        cost_estimate=pl.CostEstimate(flops=10 ** 7, bytes_accessed=10 ** 7, transcendentals=0),
        name="plan",
    )(count, pairs)


def density_call(plan, pool, own_tiles):
    tiles = pool.shape[1]
    flat = jax.ShapeDtypeStruct((own_tiles, LANES), jnp.float32)
    return pl.pallas_call(
        density_kernel,
        out_shape=(
            flat,
            flat,
            jax.ShapeDtypeStruct((tiles, LANES, FEATS), jnp.bfloat16),
            jax.ShapeDtypeStruct((5, tiles, LANES), jnp.float32),
            jax.ShapeDtypeStruct((tiles - own_tiles, LANES), jnp.int32),
            jax.ShapeDtypeStruct((1,), jnp.int32),
        ),
        in_specs=[SMEM] * 4 + [VMEM],
        out_specs=(VMEM, VMEM, VMEM, VMEM, VMEM, SMEM),
        scratch_shapes=[
            pltpu.VMEM((tiles * FEATS, LANES), jnp.float32),
            pltpu.VMEM((own_tiles, FEATS, LANES), jnp.bfloat16),
            pltpu.VMEM((tiles, LANES, LANES), jnp.float32),
            pltpu.VMEM((max(own_tiles, tiles - own_tiles) + 1, 8, LANES), jnp.float32),
        ],
        name="density",
    )(*plan, pool)


def accel_call(plan, more, far, packed, dest, press, press_far):
    own_tiles = press.shape[0]
    tiles = packed.shape[1]
    return pl.pallas_call(
        accel_kernel,
        out_shape=jax.ShapeDtypeStruct((3, own_tiles, LANES), jnp.float32),
        in_specs=[SMEM] * 5 + [VMEM] * 5,
        out_specs=VMEM,
        scratch_shapes=[
            pltpu.VMEM((tiles * FEATS, LANES), jnp.float32),
            pltpu.VMEM((own_tiles, FEATS, LANES), jnp.bfloat16),
            pltpu.VMEM((own_tiles, LANES), jnp.float32),
            pltpu.VMEM((tiles, LANES, LANES), jnp.float32),
            pltpu.VMEM((tiles, LANES), jnp.float32),
            pltpu.VMEM((own_tiles, 16, 2 * LANES), jnp.bfloat16),
            pltpu.VMEM((2, tiles - own_tiles, 16, LANES), jnp.bfloat16),
            pltpu.VMEM((own_tiles + 1, 16, LANES), jnp.float32),
        ],
        name="accel",
    )(*plan, more, far, packed, dest, press, press_far)


def local(positions, mass, smoothing, energy, destination, pairs, pair_count):
    across = lax.axis_size("gx")
    beside = lax.axis_size("gy")
    domains = across * beside
    dev_rows = mass.shape[0]
    slot_count = dev_rows // domains
    own_tiles = dev_rows // LANES
    edge_rows = GT * LANES
    plan = plan_call(pair_count, pairs, own_tiles, own_tiles + 4 * GT)
    fields = jnp.concatenate([positions, mass[None], smoothing[None], energy[None]], 0)
    ordered = lax.sort(
        (destination[:, 0],) + tuple(fields[k] for k in range(6)), num_keys=1, is_stable=True
    )
    outgoing = jnp.stack([row.reshape(domains, slot_count) for row in ordered[1:]], 1)
    outgoing = outgoing.reshape(across, beside, 6 * slot_count)
    halfway = lax.all_to_all(outgoing, "gy", split_axis=1, concat_axis=1, tiled=True)
    moved = lax.all_to_all(halfway, "gx", split_axis=0, concat_axis=0, tiled=True)
    settled = jnp.transpose(moved.reshape(domains, 6, slot_count), (1, 0, 2)).reshape(6, dev_rows)
    boundary = settled[:, :edge_rows].reshape(6, 1, 1, edge_rows)
    ghosts = extended(boundary, (("gx", 1), ("gy", 2)), 1)
    extra = neighbour_rows(ghosts)
    pool = jnp.concatenate([settled, extra], 1).reshape(6, own_tiles + 4 * GT, LANES)
    density, press, far, packed, dest, more = density_call(plan, pool, own_tiles)
    press_edge = press.reshape(-1)[:edge_rows].reshape(1, 1, edge_rows)
    press_ghosts = extended(press_edge, (("gx", 0), ("gy", 1)), 1)
    press_far = neighbour_rows(press_ghosts).reshape(4 * GT, LANES)
    accel = accel_call(plan, more, far, packed, dest, press, press_far)
    return (density.reshape(-1), accel.reshape(3, -1))


def solution(mesh):
    placed = (
        P(None, ("gx", "gy")),
        P(("gx", "gy")),
        P(("gx", "gy")),
        P(("gx", "gy")),
        P(("gx", "gy"), None),
        P(None, ("gx", "gy")),
        P(("gx", "gy")),
    )
    return jax.shard_map(
        local,
        mesh=mesh,
        in_specs=placed,
        out_specs=(P(("gx", "gy")), P(None, ("gx", "gy"))),
        check_vma=False,
    )
```

profile of v0, /device:TPU:17, one launch (start us, length us, event | category | flops | bytes accessed | tf_op | source)
XLA Modules:
  0.0 188.8 jit_solution(14646320467153055569)
XLA Ops:
  0.6 1.0 fusion.2
  1.6 7.2 %sort.63 = (s32[4096]{0:T(1024)}, f32[4096]{0:T(1024)S(1)}, f32[4096]{0:T(1024)S(1)}, f32[4096]{0:T(1024)S(1)}, f32[4096]{0:T(1024)S(1)}, /*index=5*/f32[4096]{0:T(1024)S(1)}, f32[4096]{0:T(1024)S(1)}, s32[4096]{0:T(1024)}) sort(s32[4096]{0:T(1024)} %bitcast.63, f32[4096]{0:T(1024)S(1)} %bitcast.48, f32[4096]{0:T(1024)S(1)} %bitcast.49, f32[4096]{0:T(1024)S(1)} %bitcast.47, ...), dimensions={0}, to_apply=%region_0.0 | sort | flops 49152 | bytes 262144 | tf_op jit(solution)/shard_map/sort | solution.py:428
  9.1 6.6 %all_to_all.10 = f32[8,4,768]{2,0,1:T(8,128)S(1)} all-to-all(f32[8,4,768]{2,0,1:T(8,128)S(1)} %copy.11), channel_id=1, replica_groups=mesh['gx'=8,'gy'=4] {'gy'}, dimensions={1} | all-to-all | bytes 196608 | tf_op jit(solution)/shard_map/all_to_all | solution.py:433
  15.7 0.7 copy.12
  16.3 5.6 %all-to-all-start.1 = ((f32[8,4,768]{2,1,0:T(4,128)}), f32[8,4,768]{2,1,0:T(4,128)S(1)}, u32[]{:S(2)}, u32[]{:S(2)}) async-start(f32[8,4,768]{2,1,0:T(4,128)} %copy.12), calls=%async_computation.1 | async-start | bytes 196608 | tf_op jit(solution)/shard_map/all_to_all | solution.py:434
  22.6 13.6 %plan.1 = (s32[2]{0:T(128)}, s32[865]{0:T(1024)}, s32[865]{0:T(1024)}, s32[2176]{0:T(1024)}) custom-call(s32[1]{0:T(128)S(6)} %copy.23.count_ref, s32[2,864]{1,0:T(2,128)} %pairs_ref.1), custom_call_target="tpu_custom_call" | custom-call | flops 10000000 | bytes 10000000 | tf_op jit(solution)/shard_map/plan/pallas_call | solution.py:361
  36.2 3.6 %collective-permute-start.1 = (f32[6,1,1,1024]{3,0,2,1:T(8,128)S(1)}, f32[6,1,1,1024]{3,0,2,1:T(8,128)S(1)}, u32[]{:S(2)}, u32[]{:S(2)}) collective-permute-start(f32[6,1,1,1024]{3,0,2,1:T(8,128)S(1)} %slice_bitcast_fusion.2), channel_id=1, source_target_pairs={{4,0},{8,4},{12,8},{16,12},{20,16},{24,20},{28,24},{5,1},{9,5},{13... | collective-permute-start | bytes 73736 | tf_op jit(solution)/shard_map/ppermute | solution.py:28
  39.8 1.9 %collective-permute-start = (f32[6,1,1,1024]{3,0,2,1:T(8,128)S(1)}, f32[6,1,1,1024]{3,0,2,1:T(8,128)S(1)}, u32[]{:S(2)}, u32[]{:S(2)}) collective-permute-start(f32[6,1,1,1024]{3,0,2,1:T(8,128)S(1)} %slice_bitcast_fusion.2), channel_id=1, source_target_pairs={{0,4},{4,8},{8,12},{12,16},{16,20},{20,24},{24,28},{1,5},{5,9},{9,... | collective-permute-start | bytes 73736 | tf_op jit(solution)/shard_map/ppermute | solution.py:25
  41.8 3.6 %collective-permute-done = f32[6,1,1,1024]{3,0,2,1:T(8,128)S(1)} collective-permute-done((f32[6,1,1,1024]{3,0,2,1:T(8,128)S(1)}, f32[6,1,1,1024]{3,0,2,1:T(8,128)S(1)}, u32[]{:S(2)}, u32[]{:S(2)}) %collective-permute-start) | collective-permute-done | bytes 24608 | tf_op jit(solution)/shard_map/ppermute | solution.py:25
  45.4 5.2 %collective-permute-start.3 = (f32[6,3,1,1024]{3,0,2,1:T(8,128)S(1)}, f32[6,3,1,1024]{3,0,2,1:T(8,128)S(1)}, u32[]{:S(2)}, u32[]{:S(2)}) collective-permute-start(f32[6,3,1,1024]{3,0,2,1:T(8,128)S(1)} %pad_maximum_fusion), channel_id=1, source_target_pairs={{1,0},{2,1},{3,2},{5,4},{6,5},{7,6},{9,8},{10,9},{11,10},{13,12},{... | collective-permute-start | bytes 221192 | tf_op jit(solution)/shard_map/ppermute | solution.py:28
  50.6 1.9 %collective-permute-start.2 = (f32[6,3,1,1024]{3,0,2,1:T(8,128)S(1)}, f32[6,3,1,1024]{3,0,2,1:T(8,128)S(1)}, u32[]{:S(2)}, u32[]{:S(2)}) collective-permute-start(f32[6,3,1,1024]{3,0,2,1:T(8,128)S(1)} %pad_maximum_fusion), channel_id=1, source_target_pairs={{0,1},{1,2},{2,3},{4,5},{5,6},{6,7},{8,9},{9,10},{10,11},{12,13},{... | collective-permute-start | bytes 221192 | tf_op jit(solution)/shard_map/ppermute | solution.py:25
  52.5 1.6 collective-permute-done.2
  54.1 0.7 copy.17
  54.9 42.8 %density.1 = (f32[32,128]{1,0:T(8,128)}, f32[32,128]{1,0:T(8,128)}, bf16[64,128,32]{2,1,0:T(8,128)(2,1)}, f32[5,64,128]{2,1,0:T(8,128)}, s32[32,128]{1,0:T(8,128)}, /*index=5*/s32[1]{0:T(128)}) custom-call(s32[2]{0:T(128)} %get-tuple-element.25.sizes_ref, s32[865]{0:T(1024)} %get-tuple-element.26.own_ref, s32[865]{0:T(1024)} %get-tuple-element.27.ghost_ref, ...), custom_call_target="tpu_custom_call" | custom-call | tf_op jit(solution)/shard_map/density/pallas_call | solution.py:374
  97.6 0.7 slice.34
  98.3 2.1 %collective-permute-start.5 = (f32[1,1,1024]{2,1,0:T(1,128)S(1)}, f32[1,1,1024]{2,1,0:T(1,128)S(1)}, u32[]{:S(2)}, u32[]{:S(2)}) collective-permute-start(f32[1,1,1024]{2,1,0:T(1,128)S(1)} %bitcast.56), channel_id=1, source_target_pairs={{4,0},{8,4},{12,8},{16,12},{20,16},{24,20},{28,24},{5,1},{9,5},{13... | collective-permute-start | bytes 12296 | tf_op jit(solution)/shard_map/ppermute | solution.py:28
  100.4 3.2 %collective-permute-start.4 = (f32[1,1,1024]{2,1,0:T(1,128)S(1)}, f32[1,1,1024]{2,1,0:T(1,128)S(1)}, u32[]{:S(2)}, u32[]{:S(2)}) collective-permute-start(f32[1,1,1024]{2,1,0:T(1,128)S(1)} %bitcast.57), channel_id=1, source_target_pairs={{0,4},{4,8},{8,12},{12,16},{16,20},{20,24},{24,28},{1,5},{5,9},{9,... | collective-permute-start | bytes 12296 | tf_op jit(solution)/shard_map/ppermute | solution.py:25
  103.6 2.1 %collective-permute-done.4 = f32[1,1,1024]{2,1,0:T(1,128)S(1)} collective-permute-done((f32[1,1,1024]{2,1,0:T(1,128)S(1)}, f32[1,1,1024]{2,1,0:T(1,128)S(1)}, u32[]{:S(2)}, u32[]{:S(2)}) %collective-permute-start.4) | collective-permute-done | bytes 4128 | tf_op jit(solution)/shard_map/ppermute | solution.py:25
  105.7 3.6 %collective-permute-start.7 = (f32[3,1,1024]{2,1,0:T(1,128)S(1)}, f32[3,1,1024]{2,1,0:T(1,128)S(1)}, u32[]{:S(2)}, u32[]{:S(2)}) collective-permute-start(f32[3,1,1024]{2,1,0:T(1,128)S(1)} %pad_maximum_fusion.2), channel_id=1, source_target_pairs={{1,0},{2,1},{3,2},{5,4},{6,5},{7,6},{9,8},{10,9},{11,10},{13,12},{... | collective-permute-start | bytes 36872 | tf_op jit(solution)/shard_map/ppermute | solution.py:28
  109.3 2.0 %collective-permute-start.6 = (f32[3,1,1024]{2,1,0:T(1,128)S(1)}, f32[3,1,1024]{2,1,0:T(1,128)S(1)}, u32[]{:S(2)}, u32[]{:S(2)}) collective-permute-start(f32[3,1,1024]{2,1,0:T(1,128)S(1)} %pad_maximum_fusion.2), channel_id=1, source_target_pairs={{0,1},{1,2},{2,3},{4,5},{5,6},{6,7},{8,9},{9,10},{10,11},{12,13},{... | collective-permute-start | bytes 36872 | tf_op jit(solution)/shard_map/ppermute | solution.py:25
  111.3 1.1 collective-permute-done.6
  112.4 0.6 pad_maximum_fusion.1.press_far_ref
  113.0 74.4 %accel.1 = f32[3,32,128]{2,1,0:T(8,128)} custom-call(s32[2]{0:T(128)} %get-tuple-element.25.sizes_ref, s32[865]{0:T(1024)} %get-tuple-element.26.own_ref, s32[865]{0:T(1024)} %get-tuple-element.27.ghost_ref, s32[2176]{0:T(1024)} %get-tuple-element.28.times_ref, s32[1]{0:T(128)} %get-tuple-element.36.more_ref, bf16[64,128,32]{2,1,0:T(8,128)(2,1)} %get-tuple-element.37.far, ...), custom_call_target="tpu_custom_call" | custom-call | tf_op jit(solution)/shard_map/accel/pallas_call | solution.py:399
  187.4 1.5 copy.18
  (20 shorter events, 0.3 us)
Async XLA Ops:
  16.3 19.8 %all-to-all-start.1 = ((f32[8,4,768]{2,1,0:T(4,128)}), f32[8,4,768]{2,1,0:T(4,128)S(1)}, u32[]{:S(2)}, u32[]{:S(2)}) async-start(f32[8,4,768]{2,1,0:T(4,128)} %copy.12), calls=%async_computation.1 | async-start | bytes 196608 | tf_op jit(solution)/shard_map/all_to_all | solution.py:434
  36.2 5.5 %collective-permute-start.1 = (f32[6,1,1,1024]{3,0,2,1:T(8,128)S(1)}, f32[6,1,1,1024]{3,0,2,1:T(8,128)S(1)}, u32[]{:S(2)}, u32[]{:S(2)}) collective-permute-start(f32[6,1,1,1024]{3,0,2,1:T(8,128)S(1)} %slice_bitcast_fusion.2), channel_id=1, source_target_pairs={{4,0},{8,4},{12,8},{16,12},{20,16},{24,20},{28,24},{5,1},{9,5},{13... | collective-permute-start | bytes 73736 | tf_op jit(solution)/shard_map/ppermute | solution.py:28
  39.8 5.6 %collective-permute-start = (f32[6,1,1,1024]{3,0,2,1:T(8,128)S(1)}, f32[6,1,1,1024]{3,0,2,1:T(8,128)S(1)}, u32[]{:S(2)}, u32[]{:S(2)}) collective-permute-start(f32[6,1,1,1024]{3,0,2,1:T(8,128)S(1)} %slice_bitcast_fusion.2), channel_id=1, source_target_pairs={{0,4},{4,8},{8,12},{12,16},{16,20},{20,24},{24,28},{1,5},{5,9},{9,... | collective-permute-start | bytes 73736 | tf_op jit(solution)/shard_map/ppermute | solution.py:25
  45.4 8.7 %collective-permute-start.3 = (f32[6,3,1,1024]{3,0,2,1:T(8,128)S(1)}, f32[6,3,1,1024]{3,0,2,1:T(8,128)S(1)}, u32[]{:S(2)}, u32[]{:S(2)}) collective-permute-start(f32[6,3,1,1024]{3,0,2,1:T(8,128)S(1)} %pad_maximum_fusion), channel_id=1, source_target_pairs={{1,0},{2,1},{3,2},{5,4},{6,5},{7,6},{9,8},{10,9},{11,10},{13,12},{... | collective-permute-start | bytes 221192 | tf_op jit(solution)/shard_map/ppermute | solution.py:28
  50.6 3.5 %collective-permute-start.2 = (f32[6,3,1,1024]{3,0,2,1:T(8,128)S(1)}, f32[6,3,1,1024]{3,0,2,1:T(8,128)S(1)}, u32[]{:S(2)}, u32[]{:S(2)}) collective-permute-start(f32[6,3,1,1024]{3,0,2,1:T(8,128)S(1)} %pad_maximum_fusion), channel_id=1, source_target_pairs={{0,1},{1,2},{2,3},{4,5},{5,6},{6,7},{8,9},{9,10},{10,11},{12,13},{... | collective-permute-start | bytes 221192 | tf_op jit(solution)/shard_map/ppermute | solution.py:25
  98.3 5.3 %collective-permute-start.5 = (f32[1,1,1024]{2,1,0:T(1,128)S(1)}, f32[1,1,1024]{2,1,0:T(1,128)S(1)}, u32[]{:S(2)}, u32[]{:S(2)}) collective-permute-start(f32[1,1,1024]{2,1,0:T(1,128)S(1)} %bitcast.56), channel_id=1, source_target_pairs={{4,0},{8,4},{12,8},{16,12},{20,16},{24,20},{28,24},{5,1},{9,5},{13... | collective-permute-start | bytes 12296 | tf_op jit(solution)/shard_map/ppermute | solution.py:28
  100.4 5.3 %collective-permute-start.4 = (f32[1,1,1024]{2,1,0:T(1,128)S(1)}, f32[1,1,1024]{2,1,0:T(1,128)S(1)}, u32[]{:S(2)}, u32[]{:S(2)}) collective-permute-start(f32[1,1,1024]{2,1,0:T(1,128)S(1)} %bitcast.57), channel_id=1, source_target_pairs={{0,4},{4,8},{8,12},{12,16},{16,20},{20,24},{24,28},{1,5},{5,9},{9,... | collective-permute-start | bytes 12296 | tf_op jit(solution)/shard_map/ppermute | solution.py:25
  105.7 5.6 %collective-permute-start.7 = (f32[3,1,1024]{2,1,0:T(1,128)S(1)}, f32[3,1,1024]{2,1,0:T(1,128)S(1)}, u32[]{:S(2)}, u32[]{:S(2)}) collective-permute-start(f32[3,1,1024]{2,1,0:T(1,128)S(1)} %pad_maximum_fusion.2), channel_id=1, source_target_pairs={{1,0},{2,1},{3,2},{5,4},{6,5},{7,6},{9,8},{10,9},{11,10},{13,12},{... | collective-permute-start | bytes 36872 | tf_op jit(solution)/shard_map/ppermute | solution.py:28
  109.3 3.1 %collective-permute-start.6 = (f32[3,1,1024]{2,1,0:T(1,128)S(1)}, f32[3,1,1024]{2,1,0:T(1,128)S(1)}, u32[]{:S(2)}, u32[]{:S(2)}) collective-permute-start(f32[3,1,1024]{2,1,0:T(1,128)S(1)} %pad_maximum_fusion.2), channel_id=1, source_target_pairs={{0,1},{1,2},{2,3},{4,5},{5,6},{6,7},{8,9},{9,10},{10,11},{12,13},{... | collective-permute-start | bytes 36872 | tf_op jit(solution)/shard_map/ppermute | solution.py:25
where the time goes:
time: 191 us; the launch traced here: 189 us
  Pallas kernels  131 us (69%)
  starting transfers between devices  29 us (15%)
  waiting for transfers between devices  8.36 us (4%)
  other arithmetic  7.86 us (4%)
  blocking collectives  6.58 us (3%)
  local copies, waits for them, and re-layouts  4.83 us (3%)
    pallas_call x1, Pallas kernels, accel_call(): pl.pallas_call(accel_kernel, out_shape=jax.ShapeDtypeStruct((3, own_tiles...  74.4 us
    pallas_call x1, Pallas kernels, density_call(): pl.pallas_call(density_kernel, out_shape=(flat, flat, jax.ShapeDtypeStruc...  42.8 us
    ppermute x4, starting transfers between devices, extended(): lax.ppermute(lax.slice_in_dim(block, 0, width, axis=dim), axis, backward)  14.5 us
    pallas_call x1, Pallas kernels, plan_call(): pl.pallas_call(functools.partial(plan_kernel, own_tiles=own_tiles, tiles=...  13.6 us
    ppermute x4, starting transfers between devices, extended(): lax.ppermute(lax.slice_in_dim(block, block.shape[dim] - width, None, axis...  8.96 us
    ppermute x4, waiting for transfers between devices, extended(): lax.ppermute(lax.slice_in_dim(block, block.shape[dim] - width, None, axis...  8.34 us
    sort x1, other arithmetic, local(): lax.sort((destination[:, 0],) + tuple((fields[k] for k in range(6))), num...  7.22 us
    all_to_all x1, blocking collectives, local(): lax.all_to_all(outgoing, 'gy', split_axis=1, concat_axis=1, tiled=True)  6.58 us
  transfers between devices with their start and end apart: 9, of which 4 were waited for; matrix products, arithmetic and copies ran while one was open for 0% of the time, Pallas kernels for 7%

commit v1 on v0

--- a/solution.py
+++ b/solution.py
@@ -253,8 +253,8 @@
         return body
 
     half = LANES // 2
-    sweep(own_ref, sizes_ref[0], times_ref, tiles, own_tiles, 4, add(0, LANES))
-    sweep(ghost_ref, sizes_ref[1], times_ref, tiles, own_tiles, 8, add(0, half))
+    sweep(own_ref, sizes_ref[0], times_ref, tiles, own_tiles, 8, add(0, LANES))
+    sweep(ghost_ref, sizes_ref[1], times_ref, tiles, own_tiles, 16, add(0, half))
 
     @pl.when(more > 0)
     def _():
@@ -336,8 +336,8 @@
             totals[place] += weight * jnp.dot(lhs(source), terms, preferred_element_type=jnp.float32)
         return body
 
-    sweep(own_ref, sizes_ref[0], times_ref, tiles, own_tiles, 4, add(0, LANES, lambda s: left[s]))
-    sweep(ghost_ref, sizes_ref[1], times_ref, tiles, own_tiles, 8,
+    sweep(own_ref, sizes_ref[0], times_ref, tiles, own_tiles, 8, add(0, LANES, lambda s: left[s]))
+    sweep(ghost_ref, sizes_ref[1], times_ref, tiles, own_tiles, 16,
           add(0, half, lambda s: left_half[0, jnp.maximum(s - own_tiles, 0)]))
 
     @pl.when(more_ref[0] > 0)

time: 191 us -> 172 us (0.901)
  the two profiles are of different devices: /device:TPU:17 before, /device:TPU:27 now
where the time goes in v1:
time: 172 us; the launch traced here: 170 us
  Pallas kernels  112 us (65%)
  starting transfers between devices  28.5 us (17%)
  waiting for transfers between devices  8.64 us (5%)
  other arithmetic  7.86 us (5%)
  blocking collectives  5.81 us (3%)
  local copies, waits for them, and re-layouts  4.83 us (3%)
    pallas_call x1, Pallas kernels, accel_call(): pl.pallas_call(accel_kernel, out_shape=jax.ShapeDtypeStruct((3, own_tiles...  64.4 us
    pallas_call x1, Pallas kernels, density_call(): pl.pallas_call(density_kernel, out_shape=(flat, flat, jax.ShapeDtypeStruc...  33.9 us
    ppermute x4, starting transfers between devices, extended(): lax.ppermute(lax.slice_in_dim(block, 0, width, axis=dim), axis, backward)  14.7 us
    pallas_call x1, Pallas kernels, plan_call(): pl.pallas_call(functools.partial(plan_kernel, own_tiles=own_tiles, tiles=...  14.2 us
    ppermute x4, waiting for transfers between devices, extended(): lax.ppermute(lax.slice_in_dim(block, block.shape[dim] - width, None, axis...  8.62 us
    ppermute x4, starting transfers between devices, extended(): lax.ppermute(lax.slice_in_dim(block, block.shape[dim] - width, None, axis...  8.33 us
    sort x1, other arithmetic, local(): lax.sort((destination[:, 0],) + tuple((fields[k] for k in range(6))), num...  7.22 us
    all_to_all x1, blocking collectives, local(): lax.all_to_all(outgoing, 'gy', split_axis=1, concat_axis=1, tiled=True)  5.81 us
  transfers between devices with their start and end apart: 9, of which 4 were waited for; matrix products, arithmetic and copies ran while one was open for 0% of the time, Pallas kernels for 8%

profile of v1, /device:TPU:27, one launch (start us, length us, event | category | flops | bytes accessed | tf_op | source)
XLA Modules:
  0.0 169.5 jit_solution(4328278630515691404)
XLA Ops:
  0.6 1.0 fusion.2
  1.6 7.2 %sort.63 = (s32[4096]{0:T(1024)}, f32[4096]{0:T(1024)S(1)}, f32[4096]{0:T(1024)S(1)}, f32[4096]{0:T(1024)S(1)}, f32[4096]{0:T(1024)S(1)}, /*index=5*/f32[4096]{0:T(1024)S(1)}, f32[4096]{0:T(1024)S(1)}, s32[4096]{0:T(1024)}) sort(s32[4096]{0:T(1024)} %bitcast.63, f32[4096]{0:T(1024)S(1)} %bitcast.48, f32[4096]{0:T(1024)S(1)} %bitcast.49, f32[4096]{0:T(1024)S(1)} %bitcast.47, ...), dimensions={0}, to_apply=%region_0.0 | sort | flops 49152 | bytes 262144 | tf_op jit(solution)/shard_map/sort | solution.py:428
  9.1 5.8 %all_to_all.10 = f32[8,4,768]{2,0,1:T(8,128)S(1)} all-to-all(f32[8,4,768]{2,0,1:T(8,128)S(1)} %copy.11), channel_id=1, replica_groups=mesh['gx'=8,'gy'=4] {'gy'}, dimensions={1} | all-to-all | bytes 196608 | tf_op jit(solution)/shard_map/all_to_all | solution.py:433
  14.9 0.7 copy.12
  15.6 5.5 %all-to-all-start.1 = ((f32[8,4,768]{2,1,0:T(4,128)}), f32[8,4,768]{2,1,0:T(4,128)S(1)}, u32[]{:S(2)}, u32[]{:S(2)}) async-start(f32[8,4,768]{2,1,0:T(4,128)} %copy.12), calls=%async_computation.1 | async-start | bytes 196608 | tf_op jit(solution)/shard_map/all_to_all | solution.py:434
  21.7 14.2 %plan.1 = (s32[2]{0:T(128)}, s32[865]{0:T(1024)}, s32[865]{0:T(1024)}, s32[2176]{0:T(1024)}) custom-call(s32[1]{0:T(128)S(6)} %copy.23.count_ref, s32[2,864]{1,0:T(2,128)} %pairs_ref.1), custom_call_target="tpu_custom_call" | custom-call | flops 10000000 | bytes 10000000 | tf_op jit(solution)/shard_map/plan/pallas_call | solution.py:361
  35.9 2.9 %collective-permute-start.1 = (f32[6,1,1,1024]{3,0,2,1:T(8,128)S(1)}, f32[6,1,1,1024]{3,0,2,1:T(8,128)S(1)}, u32[]{:S(2)}, u32[]{:S(2)}) collective-permute-start(f32[6,1,1,1024]{3,0,2,1:T(8,128)S(1)} %slice_bitcast_fusion.2), channel_id=1, source_target_pairs={{4,0},{8,4},{12,8},{16,12},{20,16},{24,20},{28,24},{5,1},{9,5},{13... | collective-permute-start | bytes 73736 | tf_op jit(solution)/shard_map/ppermute | solution.py:28
  38.8 2.4 %collective-permute-start = (f32[6,1,1,1024]{3,0,2,1:T(8,128)S(1)}, f32[6,1,1,1024]{3,0,2,1:T(8,128)S(1)}, u32[]{:S(2)}, u32[]{:S(2)}) collective-permute-start(f32[6,1,1,1024]{3,0,2,1:T(8,128)S(1)} %slice_bitcast_fusion.2), channel_id=1, source_target_pairs={{0,4},{4,8},{8,12},{12,16},{16,20},{20,24},{24,28},{1,5},{5,9},{9,... | collective-permute-start | bytes 73736 | tf_op jit(solution)/shard_map/ppermute | solution.py:25
  41.3 3.1 %collective-permute-done = f32[6,1,1,1024]{3,0,2,1:T(8,128)S(1)} collective-permute-done((f32[6,1,1,1024]{3,0,2,1:T(8,128)S(1)}, f32[6,1,1,1024]{3,0,2,1:T(8,128)S(1)}, u32[]{:S(2)}, u32[]{:S(2)}) %collective-permute-start) | collective-permute-done | bytes 24608 | tf_op jit(solution)/shard_map/ppermute | solution.py:25
  44.4 3.3 %collective-permute-start.3 = (f32[6,3,1,1024]{3,0,2,1:T(8,128)S(1)}, f32[6,3,1,1024]{3,0,2,1:T(8,128)S(1)}, u32[]{:S(2)}, u32[]{:S(2)}) collective-permute-start(f32[6,3,1,1024]{3,0,2,1:T(8,128)S(1)} %pad_maximum_fusion), channel_id=1, source_target_pairs={{1,0},{2,1},{3,2},{5,4},{6,5},{7,6},{9,8},{10,9},{11,10},{13,12},{... | collective-permute-start | bytes 221192 | tf_op jit(solution)/shard_map/ppermute | solution.py:28
  47.8 1.3 collective-permute-start.2
  49.1 1.9 %collective-permute-done.2 = f32[6,3,1,1024]{3,0,2,1:T(8,128)S(1)} collective-permute-done((f32[6,3,1,1024]{3,0,2,1:T(8,128)S(1)}, f32[6,3,1,1024]{3,0,2,1:T(8,128)S(1)}, u32[]{:S(2)}, u32[]{:S(2)}) %collective-permute-start.2) | collective-permute-done | bytes 73760 | tf_op jit(solution)/shard_map/ppermute | solution.py:25
  51.0 0.7 copy.17
  51.7 33.9 %density.1 = (f32[32,128]{1,0:T(8,128)}, f32[32,128]{1,0:T(8,128)}, bf16[64,128,32]{2,1,0:T(8,128)(2,1)}, f32[5,64,128]{2,1,0:T(8,128)}, s32[32,128]{1,0:T(8,128)}, /*index=5*/s32[1]{0:T(128)}) custom-call(s32[2]{0:T(128)} %get-tuple-element.25.sizes_ref, s32[865]{0:T(1024)} %get-tuple-element.26.own_ref, s32[865]{0:T(1024)} %get-tuple-element.27.ghost_ref, ...), custom_call_target="tpu_custom_call" | custom-call | tf_op jit(solution)/shard_map/density/pallas_call | solution.py:374
  85.6 0.7 slice.34
  86.3 1.9 %collective-permute-start.5 = (f32[1,1,1024]{2,1,0:T(1,128)S(1)}, f32[1,1,1024]{2,1,0:T(1,128)S(1)}, u32[]{:S(2)}, u32[]{:S(2)}) collective-permute-start(f32[1,1,1024]{2,1,0:T(1,128)S(1)} %bitcast.56), channel_id=1, source_target_pairs={{4,0},{8,4},{12,8},{16,12},{20,16},{24,20},{28,24},{5,1},{9,5},{13... | collective-permute-start | bytes 12296 | tf_op jit(solution)/shard_map/ppermute | solution.py:28
  88.2 3.4 %collective-permute-start.4 = (f32[1,1,1024]{2,1,0:T(1,128)S(1)}, f32[1,1,1024]{2,1,0:T(1,128)S(1)}, u32[]{:S(2)}, u32[]{:S(2)}) collective-permute-start(f32[1,1,1024]{2,1,0:T(1,128)S(1)} %bitcast.57), channel_id=1, source_target_pairs={{0,4},{4,8},{8,12},{12,16},{16,20},{20,24},{24,28},{1,5},{5,9},{9,... | collective-permute-start | bytes 12296 | tf_op jit(solution)/shard_map/ppermute | solution.py:25
  91.6 1.9 %collective-permute-done.4 = f32[1,1,1024]{2,1,0:T(1,128)S(1)} collective-permute-done((f32[1,1,1024]{2,1,0:T(1,128)S(1)}, f32[1,1,1024]{2,1,0:T(1,128)S(1)}, u32[]{:S(2)}, u32[]{:S(2)}) %collective-permute-start.4) | collective-permute-done | bytes 4128 | tf_op jit(solution)/shard_map/ppermute | solution.py:25
  93.5 6.5 %collective-permute-start.7 = (f32[3,1,1024]{2,1,0:T(1,128)S(1)}, f32[3,1,1024]{2,1,0:T(1,128)S(1)}, u32[]{:S(2)}, u32[]{:S(2)}) collective-permute-start(f32[3,1,1024]{2,1,0:T(1,128)S(1)} %pad_maximum_fusion.2), channel_id=1, source_target_pairs={{1,0},{2,1},{3,2},{5,4},{6,5},{7,6},{9,8},{10,9},{11,10},{13,12},{... | collective-permute-start | bytes 36872 | tf_op jit(solution)/shard_map/ppermute | solution.py:28
  100.0 1.3 collective-permute-start.6
  101.3 1.8 %collective-permute-done.6 = f32[3,1,1024]{2,1,0:T(1,128)S(1)} collective-permute-done((f32[3,1,1024]{2,1,0:T(1,128)S(1)}, f32[3,1,1024]{2,1,0:T(1,128)S(1)}, u32[]{:S(2)}, u32[]{:S(2)}) %collective-permute-start.6) | collective-permute-done | bytes 12320 | tf_op jit(solution)/shard_map/ppermute | solution.py:25
  103.1 0.6 pad_maximum_fusion.1.press_far_ref
  103.7 64.4 %accel.1 = f32[3,32,128]{2,1,0:T(8,128)} custom-call(s32[2]{0:T(128)} %get-tuple-element.25.sizes_ref, s32[865]{0:T(1024)} %get-tuple-element.26.own_ref, s32[865]{0:T(1024)} %get-tuple-element.27.ghost_ref, s32[2176]{0:T(1024)} %get-tuple-element.28.times_ref, s32[1]{0:T(128)} %get-tuple-element.36.more_ref, bf16[64,128,32]{2,1,0:T(8,128)(2,1)} %get-tuple-element.37.far, ...), custom_call_target="tpu_custom_call" | custom-call | tf_op jit(solution)/shard_map/accel/pallas_call | solution.py:399
  168.1 1.5 copy.18
  (20 shorter events, 0.3 us)
Async XLA Ops:
  15.6 20.3 %all-to-all-start.1 = ((f32[8,4,768]{2,1,0:T(4,128)}), f32[8,4,768]{2,1,0:T(4,128)S(1)}, u32[]{:S(2)}, u32[]{:S(2)}) async-start(f32[8,4,768]{2,1,0:T(4,128)} %copy.12), calls=%async_computation.1 | async-start | bytes 196608 | tf_op jit(solution)/shard_map/all_to_all | solution.py:434
  35.9 5.3 %collective-permute-start.1 = (f32[6,1,1,1024]{3,0,2,1:T(8,128)S(1)}, f32[6,1,1,1024]{3,0,2,1:T(8,128)S(1)}, u32[]{:S(2)}, u32[]{:S(2)}) collective-permute-start(f32[6,1,1,1024]{3,0,2,1:T(8,128)S(1)} %slice_bitcast_fusion.2), channel_id=1, source_target_pairs={{4,0},{8,4},{12,8},{16,12},{20,16},{24,20},{28,24},{5,1},{9,5},{13... | collective-permute-start | bytes 73736 | tf_op jit(solution)/shard_map/ppermute | solution.py:28
  38.8 5.6 %collective-permute-start = (f32[6,1,1,1024]{3,0,2,1:T(8,128)S(1)}, f32[6,1,1,1024]{3,0,2,1:T(8,128)S(1)}, u32[]{:S(2)}, u32[]{:S(2)}) collective-permute-start(f32[6,1,1,1024]{3,0,2,1:T(8,128)S(1)} %slice_bitcast_fusion.2), channel_id=1, source_target_pairs={{0,4},{4,8},{8,12},{12,16},{16,20},{20,24},{24,28},{1,5},{5,9},{9,... | collective-permute-start | bytes 73736 | tf_op jit(solution)/shard_map/ppermute | solution.py:25
  44.4 6.5 %collective-permute-start.3 = (f32[6,3,1,1024]{3,0,2,1:T(8,128)S(1)}, f32[6,3,1,1024]{3,0,2,1:T(8,128)S(1)}, u32[]{:S(2)}, u32[]{:S(2)}) collective-permute-start(f32[6,3,1,1024]{3,0,2,1:T(8,128)S(1)} %pad_maximum_fusion), channel_id=1, source_target_pairs={{1,0},{2,1},{3,2},{5,4},{6,5},{7,6},{9,8},{10,9},{11,10},{13,12},{... | collective-permute-start | bytes 221192 | tf_op jit(solution)/shard_map/ppermute | solution.py:28
  47.8 3.2 %collective-permute-start.2 = (f32[6,3,1,1024]{3,0,2,1:T(8,128)S(1)}, f32[6,3,1,1024]{3,0,2,1:T(8,128)S(1)}, u32[]{:S(2)}, u32[]{:S(2)}) collective-permute-start(f32[6,3,1,1024]{3,0,2,1:T(8,128)S(1)} %pad_maximum_fusion), channel_id=1, source_target_pairs={{0,1},{1,2},{2,3},{4,5},{5,6},{6,7},{8,9},{9,10},{10,11},{12,13},{... | collective-permute-start | bytes 221192 | tf_op jit(solution)/shard_map/ppermute | solution.py:25
  86.3 5.3 %collective-permute-start.5 = (f32[1,1,1024]{2,1,0:T(1,128)S(1)}, f32[1,1,1024]{2,1,0:T(1,128)S(1)}, u32[]{:S(2)}, u32[]{:S(2)}) collective-permute-start(f32[1,1,1024]{2,1,0:T(1,128)S(1)} %bitcast.56), channel_id=1, source_target_pairs={{4,0},{8,4},{12,8},{16,12},{20,16},{24,20},{28,24},{5,1},{9,5},{13... | collective-permute-start | bytes 12296 | tf_op jit(solution)/shard_map/ppermute | solution.py:28
  88.2 5.3 %collective-permute-start.4 = (f32[1,1,1024]{2,1,0:T(1,128)S(1)}, f32[1,1,1024]{2,1,0:T(1,128)S(1)}, u32[]{:S(2)}, u32[]{:S(2)}) collective-permute-start(f32[1,1,1024]{2,1,0:T(1,128)S(1)} %bitcast.57), channel_id=1, source_target_pairs={{0,4},{4,8},{8,12},{12,16},{16,20},{20,24},{24,28},{1,5},{5,9},{9,... | collective-permute-start | bytes 12296 | tf_op jit(solution)/shard_map/ppermute | solution.py:25
  93.5 7.8 %collective-permute-start.7 = (f32[3,1,1024]{2,1,0:T(1,128)S(1)}, f32[3,1,1024]{2,1,0:T(1,128)S(1)}, u32[]{:S(2)}, u32[]{:S(2)}) collective-permute-start(f32[3,1,1024]{2,1,0:T(1,128)S(1)} %pad_maximum_fusion.2), channel_id=1, source_target_pairs={{1,0},{2,1},{3,2},{5,4},{6,5},{7,6},{9,8},{10,9},{11,10},{13,12},{... | collective-permute-start | bytes 36872 | tf_op jit(solution)/shard_map/ppermute | solution.py:28
  100.0 3.1 %collective-permute-start.6 = (f32[3,1,1024]{2,1,0:T(1,128)S(1)}, f32[3,1,1024]{2,1,0:T(1,128)S(1)}, u32[]{:S(2)}, u32[]{:S(2)}) collective-permute-start(f32[3,1,1024]{2,1,0:T(1,128)S(1)} %pad_maximum_fusion.2), channel_id=1, source_target_pairs={{0,1},{1,2},{2,3},{4,5},{5,6},{6,7},{8,9},{9,10},{10,11},{12,13},{... | collective-permute-start | bytes 36872 | tf_op jit(solution)/shard_map/ppermute | solution.py:25
